TPU v7x, 32 devices: a whole 2x2x4 slice. The times are simulated.
32 devices in a mesh: group: 8 (over z, x), sub: 4 (over y, core).
Axes of the slice: x: 2, y: 2, z: 4, core: 2. Of those that a mesh axis runs over, the one named last changes fastest.
Arguments:
- embeddings: bfloat16 [65536, 768], P(('group', 'sub'))
- labels: int32 [512], P(('group', 'sub')), may hold values from 0 to 1, as said below
- group_bit: int32 [1], replicated, may hold values from 0 to 2
- init_index: int32 [8, 128], P('group'), may hold values from 0 to 8191
Outputs:
- centroids: float32 [8, 128, 768], P('group')
- counts: float32 [8, 128], P('group')
Inputs may be any that keep to these rules, and one draw needn't show every extreme that they name: `labels`: each label is a child, 0 or 1. `init_index`: row numbers within group g, counted along the sub axis in order.
All inputs are finite; a program needn't handle non-finite values.
Results may differ from a plain program's by a relative error of at most 0.0031.
Values may be sent and summed in bfloat16 or wider, within the bound.
No kernel may reach another device: no remote copies, remote signals or barrier semaphores. Data moves between devices by JAX's collectives and lax.ppermute only.
A program may use at most 64 MiB of HBM per device.

v0:
```python
from functools import partial

import jax
import jax.numpy as jnp
from jax import lax
from jax.experimental import pallas as pl
from jax.experimental.pallas import tpu as pltpu
from jax.sharding import PartitionSpec as P

ITERS = 2
PRIOR = 1.0
CORES = 2
TAIL = 8
LANES = 128
SEED_VMEM = 60 << 20
CHUNKS = 4
OUT_CHUNKS = 4
BF16, F32 = jnp.bfloat16, jnp.float32
AXES = ("group", "sub")
VMEM = pl.BlockSpec(memory_space=pltpu.VMEM)
HBM = pl.BlockSpec(memory_space=pltpu.HBM)


def contract(a, b, dim_a, dim_b):
    return lax.dot_general(a, b, (((dim_a,), (dim_b,)), ((), ())), preferred_element_type=F32)


def column(row):
    k = row.shape[1]
    diagonal = lax.broadcasted_iota(jnp.int32, (k, k), 0) == lax.broadcasted_iota(jnp.int32, (k, k), 1)
    return jnp.sum(jnp.where(diagonal, row, jnp.zeros_like(row)), axis=1, keepdims=True)


def halves(number):
    high = number.astype(BF16).astype(F32)
    return jnp.where(lax.broadcasted_iota(jnp.int32, number.shape, 0) == 0, high, number - high).astype(BF16)


def tree(terms):
    while len(terms) > 1:
        terms = [terms[i] + terms[i + 1] for i in range(0, len(terms), 2)]
    return terms[0]


def seed_kernel(index_ref, labels_ref, rows_ref, out_ref, held_ref, index, labels, sems):
    chunks = sems.shape[0] - 2
    k, width = index_ref.shape[1], rows_ref.shape[1]
    rows = rows_ref.shape[0]
    size = rows // chunks
    first = pltpu.make_async_copy(index_ref, index, sems.at[chunks])
    first.start()
    second = pltpu.make_async_copy(labels_ref, labels, sems.at[chunks + 1])
    second.start()
    copies = []
    for i in range(chunks):
        span = pl.ds(i * size, size)
        copies.append(pltpu.make_async_copy(rows_ref.at[span], held_ref.at[span], sems.at[i]))
        copies[-1].start()
    first.wait()
    picked = column(index[...].astype(F32)).astype(jnp.int32) - lax.axis_index("sub") * rows
    total = jnp.zeros((k, width), F32)
    for i in range(chunks):
        onehot = (lax.broadcasted_iota(jnp.int32, (k, size), 1) == picked - i * size).astype(F32).astype(BF16)
        copies[i].wait()
        total = total + contract(onehot, held_ref[pl.ds(i * size, size), :], 1, 0)
    out_ref[0:k, :] = total.astype(BF16)
    out_ref[k : k + TAIL, :] = jnp.zeros((TAIL, width), BF16)
    second.wait()
    marks = jnp.concatenate([labels[...].astype(F32), jnp.zeros((1, LANES - labels.shape[1]), F32)], axis=1)
    out_ref[k : k + TAIL, 0:LANES] = jnp.broadcast_to(marks, (TAIL, LANES)).astype(BF16)


def hold_kernel(half, block, rows_ref, marks_ref, *refs):
    held_ref, turned_ref, kept_ref = refs[-3:]
    size = rows_ref.shape[0] // 4

    @pl.loop(0, 4)
    def _(i):
        span = pl.ds(pl.multiple_of(i * size, size), size)
        part = rows_ref[span, :]
        held_ref[half, span, :] = part
        turned_ref[half, :, span] = part.T

    core = lax.rem(lax.axis_index("sub"), CORES)
    k = marks_ref.shape[0] - TAIL
    chosen = (marks_ref[k : k + 1, 0:LANES].astype(F32) == core.astype(F32)).astype(F32)
    wide = [jnp.broadcast_to(chosen[:, j : j + 1], (1, block)) for j in range(rows_ref.shape[0] // block)]
    kept_ref[half] = jnp.broadcast_to(jnp.concatenate(wide, axis=1), kept_ref.shape[1:])


def accumulate(half, held_ref, turned_ref, kept_ref, out_ref, sums, counts, scale, unroll):
    k, width = half.shape
    rows = held_ref.shape[1]
    square = half.astype(F32)
    norms = jnp.sum(square * square, axis=1, keepdims=True)

    @pl.loop(0, CORES, unroll=unroll)
    def _(i):
        logits = (2.0 * contract(half, turned_ref[i], 1, 0) - norms) * (1.0 / scale)
        top = jnp.max(logits, axis=0, keepdims=True)
        e = jnp.exp(logits - top)
        weights = (e * (1.0 / jnp.sum(e, axis=0, keepdims=True))).astype(BF16)
        weights = weights * kept_ref[i, 0:1, :].astype(BF16)
        sums[i] = contract(weights, held_ref[i], 1, 0)
        counts[i] = contract(jnp.ones((TAIL, rows), BF16), weights, 1, 1)

    out_ref[0:k, :] = (sums[0] + sums[1]).astype(BF16)
    out_ref[k : k + TAIL, :] = jnp.zeros((TAIL, width), BF16)
    out_ref[k : k + TAIL, 0:k] = halves(counts[0] + counts[1])


def owner(bit):
    side = jnp.bitwise_and(jnp.right_shift(lax.axis_index("group"), bit), 1)
    return lax.rem(lax.axis_index("sub"), CORES) == side


def first_kernel(bit, scale, n, *refs):
    own_marks, other_marks = refs[:2]
    parts = refs[2 : 2 + n]
    held, turned, kept, out_ref, c_ref, sums, counts = refs[2 + n :]
    k = c_ref.shape[0]
    chip = own_marks[0:k, :].astype(F32) + other_marks[0:k, :].astype(F32)
    centroids = jnp.where(owner(bit), chip, parts[-1][0:k, :].astype(F32))
    for part in parts[:-1]:
        centroids = centroids + part[0:k, :].astype(F32)
    half = centroids.astype(BF16)
    c_ref[...] = half
    accumulate(half, held, turned, kept, out_ref, sums, counts, scale, False)


def number_of(tail):
    return tail[0:1, :] + tail[1:2, :]


def next_kernel(scale, before_ref, one, two, held, turned, kept, out_ref, c_ref, sums, counts):
    k = c_ref.shape[0]
    tail = one[k : k + TAIL, 0:k].astype(F32) + two[k : k + TAIL, 0:k].astype(F32)
    total = one[0:k, :].astype(F32) + two[0:k, :].astype(F32)
    centroids = (total + PRIOR * before_ref[...].astype(F32)) * (1.0 / (column(number_of(tail)) + PRIOR))
    c_ref[...] = centroids
    accumulate(centroids.astype(BF16), held, turned, kept, out_ref, sums, counts, scale, True)


def merge_kernel(one, two, out_ref):
    k = one.shape[0] - TAIL
    out_ref[0:k, :] = (one[0:k, :].astype(F32) + two[0:k, :].astype(F32)).astype(BF16)
    tail = one[k : k + TAIL, :].astype(F32) + two[k : k + TAIL, :].astype(F32)
    out_ref[k : k + TAIL, :] = halves(jnp.broadcast_to(number_of(tail), tail.shape))


def share_kernel(bit, before_ref, *refs):
    parts, out_ref = refs[:-1], refs[-1]
    k = before_ref.shape[0]
    mine = owner(bit)
    wide = [part[...].astype(F32) for part in parts]
    if len(parts) == 3:
        chip = lax.axis_index("sub") // CORES
        own, hub_0, hub_1 = wide
        near, far = jnp.where(chip == 0, hub_0, hub_1), jnp.where(chip == 0, hub_1, hub_0)
        total = jnp.where(mine, (own + far) + near, near)
    else:
        total = tree(wide)
        total = jnp.where(mine, total, jnp.zeros_like(total))
    before = PRIOR * before_ref[...]
    out_ref[0:k, :] = total[0:k, :] + jnp.where(mine, before, jnp.zeros_like(before))
    tail = total[k : k + TAIL, :]
    out_ref[k : k + TAIL, :] = jnp.broadcast_to(number_of(tail), tail.shape)


def output_kernel(one, two, out_ref, number_ref, held, row, sems):
    k = held.shape[0]
    number = one[k : k + 1, 0:k] + two[k : k + 1, 0:k]
    row[...] = number
    copies = [pltpu.make_async_copy(row, number_ref, sems.at[OUT_CHUNKS])]
    copies[0].start()
    factor = 1.0 / (column(number) + PRIOR)
    size = k // OUT_CHUNKS
    for i in range(OUT_CHUNKS):
        span = pl.ds(i * size, size)
        held[span, :] = (one[span, :] + two[span, :]) * factor[i * size : (i + 1) * size]
        copies.append(pltpu.make_async_copy(held.at[span], out_ref.at[0, span], sems.at[i]))
        copies[-1].start()
    for copy in copies:
        copy.wait()


def call(kernel, ins, outs, out_specs=VMEM, scratch=(), flops=0, limit=28 << 20, aliases=None):
    return pl.pallas_call(
        kernel,
        out_shape=outs,
        in_specs=ins,
        out_specs=out_specs,
        scratch_shapes=list(scratch),
        input_output_aliases=aliases or {},
        compiler_params=pltpu.CompilerParams(vmem_limit_bytes=limit),
        cost_estimate=pl.CostEstimate(flops=flops, bytes_accessed=1 << 20, transcendentals=0),
    )


class Plan:
    def __init__(self, bit):
        self.mask = 1 << bit
        self.groups = lax.axis_size("group")
        self.subs = lax.axis_size("sub")
        self.chips = self.subs // CORES
        self.bit = bit

    def devices(self):
        for group in range(self.groups):
            for sub in range(self.subs):
                yield group, sub // CORES, sub % CORES, (group >> self.bit) & 1

    def flat(self, group, chip, core):
        return group * self.subs + chip * CORES + core

    def permute(self, value, target):
        pairs = [(self.flat(*device[:3]), self.flat(*target(*device))) for device in self.devices()]
        return lax.ppermute(value, AXES, pairs)

    def seeds(self, value):
        received = []
        for step in range(1, self.chips):
            received.append(
                self.permute(
                    value,
                    lambda group, chip, core, side: (
                        (group, chip ^ step, core)
                        if core == side
                        else (group ^ self.mask, chip ^ (step - 1), 1 - core)
                    ),
                )
            )
        received.append(
            self.permute(
                value,
                lambda group, chip, core, side: (
                    (group ^ self.mask, chip ^ (self.chips - 1), core) if core == side else (group, chip, 1 - core)
                ),
            )
        )
        return received

    def sums(self, value):
        moves = [(0, 1 << i) for i in range(self.chips.bit_length() - 1)]
        orders = [moves + [(self.mask, 0)], [(self.mask, 0)] + moves]
        for i in range(len(moves) + 1):
            if i:
                value = merge(*pair)

            def target(group, chip, core, side):
                flip, step = orders[core][i]
                return group ^ flip, chip ^ step, core

            pair = value, self.permute(value, target)
        return pair

    def last_sums(self, value):
        received = [value]
        if self.chips == 2:
            for hub in (0, 1):

                def target(group, chip, core, side):
                    if core != side:
                        return group ^ self.mask, hub, core if chip == 0 else 1 - core
                    return group, 1 - hub, core if chip == hub else 1 - core

                received.append(self.permute(value, target))
            return received
        for step in range(1, self.chips):
            received.append(self.permute(value, lambda group, chip, core, side: (group, chip ^ step, core)))
        for step in range(self.chips):
            received.append(
                self.permute(
                    value,
                    lambda group, chip, core, side: (
                        (group, chip, 1 - core) if core == side else (group ^ self.mask, chip ^ step, core)
                    ),
                )
            )
        return received


def merge(own, other):
    return call(merge_kernel, [VMEM] * 2, jax.ShapeDtypeStruct(own.shape, own.dtype))(own, other)


def swap_cores(value):
    return lax.ppermute(value, "sub", [(sub, sub ^ 1) for sub in range(lax.axis_size("sub"))])


def refine(own_marks, other_marks, own_rows, bit, block):
    plan = Plan(bit)
    other_rows = swap_cores(own_rows)
    rows = own_rows.shape[0]
    k, width = own_marks.shape[0] - TAIL, own_marks.shape[1]
    scale = width / 8.0
    scratch = [
        pltpu.VMEM((CORES, k, width), F32), pltpu.VMEM((CORES, TAIL, k), F32)
    ]
    flops = 8 * rows * k * width

    both = [
        jax.ShapeDtypeStruct((CORES, rows, width), BF16),
        jax.ShapeDtypeStruct((CORES, width, rows), BF16),
        jax.ShapeDtypeStruct((CORES, TAIL, rows), F32),
    ]
    held = call(partial(hold_kernel, 0, block), [VMEM] * 2, both, [VMEM] * 3)(own_rows, own_marks)
    held = call(
        partial(hold_kernel, 1, block), [VMEM] * 5, both, [VMEM] * 3, aliases={2: 0, 3: 1, 4: 2}
    )(other_rows, other_marks, *held)
    payload = jax.ShapeDtypeStruct((k + TAIL, width), BF16)

    def iteration(kernel, inputs, kept):
        return call(
            kernel, [VMEM] * (len(inputs) + len(held)), (payload, jax.ShapeDtypeStruct((k, width), kept)), (VMEM, VMEM),
            scratch, flops,
        )(*inputs, *held)

    seeds = plan.seeds((own_marks + other_marks)[0:k])
    sums, centroids = iteration(
        partial(first_kernel, bit, scale, len(seeds)), [own_marks, other_marks, *seeds], BF16
    )
    for _ in range(ITERS - 1):
        sums, centroids = iteration(
            partial(next_kernel, scale), [centroids, *plan.sums(sums)], F32
        )
    parts = plan.last_sums(sums)
    return call(
        partial(share_kernel, bit), [VMEM] * (1 + len(parts)), jax.ShapeDtypeStruct((k + TAIL, width), F32)
    )(centroids, *parts)


def local(embeddings, labels, group_bit, init_index):
    k, width = init_index.shape[1], embeddings.shape[1]
    rows = embeddings.shape[0]
    levels = lax.axis_size("group").bit_length() - 1
    own_marks, own_rows = call(
        seed_kernel, [HBM] * 3,
        (jax.ShapeDtypeStruct((k + TAIL, width), BF16), jax.ShapeDtypeStruct((rows, width), BF16)), (VMEM, VMEM),
        [
            pltpu.VMEM((1, k), jnp.int32),
            pltpu.VMEM((1, labels.shape[0]), jnp.int32),
            pltpu.SemaphoreType.DMA((CHUNKS + 2,)),
        ], 2 * k * rows * width, SEED_VMEM,
    )(init_index, labels[None], embeddings)
    other_marks = swap_cores(own_marks)
    block = rows // labels.shape[0]
    share = lax.switch(
        group_bit[0],
        [partial(refine, bit=bit, block=block) for bit in range(levels)],
        own_marks, other_marks, own_rows,
    )
    return call(
        output_kernel, [VMEM] * 2,
        (jax.ShapeDtypeStruct((1, k, width), F32), jax.ShapeDtypeStruct((1, k), F32)), (HBM, HBM),
        [pltpu.VMEM((k, width), F32), pltpu.VMEM((1, k), F32), pltpu.SemaphoreType.DMA((OUT_CHUNKS + 1,))],
    )(share, swap_cores(share))


def solution(mesh):
    return jax.shard_map(
        local,
        mesh=mesh,
        in_specs=(P(("group", "sub"), None), P(("group", "sub")), P(), P("group", None)),
        out_specs=(P("group", None, None), P("group", None)),
        check_vma=False,
    )
```

profile of v0, /device:TPU:0, one launch (start us, length us, event | category | flops | bytes accessed | tf_op | source)
XLA Modules:
  0.0 42.3 jit_solution(4199748628484961812)
XLA Ops:
  0.6 2.3 %shard_map.59 = (bf16[136,768]{1,0:T(8,128)(2,1)S(1)}, bf16[2048,768]{1,0:T(8,128)(2,1)S(1)}) custom-call(s32[1,128]{1,0:T(1,128)} %index_ref.1, s32[1,16]{1,0:T(1,128)} %bitcast.2, bf16[2048,768]{1,0:T(8,128)(2,1)} %rows_ref.1), custom_call_target="tpu_custom_call" | custom-call | flops 402653184 | bytes 1048576 | tf_op jit(solution)/shard_map/pallas_call | solution.py:337
  3.0 0.5 %collective-permute-start.21 = (bf16[136,768]{1,0:T(8,128)(2,1)S(1)}, bf16[136,768]{1,0:T(8,128)(2,1)S(1)}, u32[]{:S(2)}, u32[]{:S(2)}) collective-permute-start(bf16[136,768]{1,0:T(8,128)(2,1)S(1)} %get-tuple-element.65), channel_id=1, source_target_pairs={{0,1},{1,0},{2,3},{3,2},{4,5},{5,4},{6,7},{7,6},{8,9},{9,8},{10,11... | collective-permute-start | bytes 626696 | tf_op jit(solution)/shard_map/ppermute | solution.py:288
  4.1 0.4 %collective-permute-done.21 = bf16[136,768]{1,0:T(8,128)(2,1)S(1)} collective-permute-done((bf16[136,768]{1,0:T(8,128)(2,1)S(1)}, bf16[136,768]{1,0:T(8,128)(2,1)S(1)}, u32[]{:S(2)}, u32[]{:S(2)}) %collective-permute-start.21) | collective-permute-done | bytes 208928 | tf_op jit(solution)/shard_map/ppermute | solution.py:288
  4.6 34.8 %conditional.1 = (f32[136,768]{1,0:T(8,128)S(1)}) conditional(s32[]{:T(128)} %bitcast, (bf16[136,768]{1,0:T(8,128)(2,1)S(1)}, bf16[136,768]{1,0:T(8,128)(2,1)S(1)}, bf16[2048,768]{1,0:T(8,128)(2,1)S(1)}) %tuple.16, (bf16[136,768]{1,0:T(8,128)(2,1)S(1)}, bf16[136,768]{1,0:T(8,128)(2,1)S(1)}, ...), branch_computations={%region_0.0_spmd, %region_1.0_spmd, %region_2.0_spmd} | conditional | flops 3221323776 | bytes 24379680 | solution.py:348
  4.6 0.4 collective-permute-start.2
  5.0 2.7 %collective-permute-start = (bf16[128,768]{1,0:T(8,128)(2,1)S(1)}, bf16[128,768]{1,0:T(8,128)(2,1)S(1)}, u32[]{:S(2)}, u32[]{:S(2)}) collective-permute-start(bf16[128,768]{1,0:T(8,128)(2,1)S(1)} %slice_add_fusion), channel_id=1, source_target_pairs={{0,2},{1,4},{2,0},{3,6},{4,1},{5,7},{6,3},{7,5},{8,10},{9,12},{10,... | collective-permute-start | bytes 589832 | tf_op jit(solution)/shard_map/cond/branch_0_fun/ppermute | solution.py:218
  7.7 1.4 %collective-permute-start.1 = (bf16[128,768]{1,0:T(8,128)(2,1)S(1)}, bf16[128,768]{1,0:T(8,128)(2,1)S(1)}, u32[]{:S(2)}, u32[]{:S(2)}) collective-permute-start(bf16[128,768]{1,0:T(8,128)(2,1)S(1)} %slice_add_fusion), channel_id=1, source_target_pairs={{0,6},{1,0},{2,4},{3,2},{4,5},{5,3},{6,7},{7,1},{8,14},{9,8},{10,1... | collective-permute-start | bytes 589832 | tf_op jit(solution)/shard_map/cond/branch_0_fun/ppermute | solution.py:218
  9.1 1.2 %branch_0_fun.6 = (bf16[2,2048,768]{2,1,0:T(8,128)(2,1)S(1)}, bf16[2,768,2048]{2,1,0:T(8,128)(2,1)S(1)}, f32[2,8,2048]{2,1,0:T(8,128)S(1)}) custom-call(bf16[2048,768]{1,0:T(8,128)(2,1)S(1)} %get-tuple-element.24.rows_ref, bf16[136,768]{1,0:T(8,128)(2,1)S(1)} %get-tuple-element.18.marks_ref.refs_0_), custom_call_target="tpu_custom_call" | custom-call | bytes 1048576 | tf_op jit(solution)/shard_map/cond/branch_0_fun/pallas_call | solution.py:307
  10.3 0.0 collective-permute-done.2.rows_ref
  10.3 1.2 %branch_0_fun.7 = (bf16[2,2048,768]{2,1,0:T(8,128)(2,1)S(1)}, bf16[2,768,2048]{2,1,0:T(8,128)(2,1)S(1)}, f32[2,8,2048]{2,1,0:T(8,128)S(1)}) custom-call(bf16[2048,768]{1,0:T(8,128)(2,1)S(1)} %collective-permute-done.2.rows_ref, bf16[136,768]{1,0:T(8,128)(2,1)S(1)} %get-tuple-element.19.marks_ref.refs_1_, ...), custom_call_target="tpu_custom_call", output_to_operand_aliasing={{0}: (2, {}), {1}: (3, {}), {2}: (4, {})} | custom-call | bytes 1048576 | tf_op jit(solution)/shard_map/cond/branch_0_fun/pallas_call | solution.py:308
  11.6 1.5 %collective-permute-done.refs_2_ = bf16[128,768]{1,0:T(8,128)(2,1)S(1)} collective-permute-done((bf16[128,768]{1,0:T(8,128)(2,1)S(1)}, bf16[128,768]{1,0:T(8,128)(2,1)S(1)}, u32[]{:S(2)}, u32[]{:S(2)}) %collective-permute-start) | collective-permute-done | bytes 196640 | tf_op jit(solution)/shard_map/cond/branch_0_fun/ppermute | solution.py:218
  13.0 0.0 collective-permute-done.1.refs_3_
  13.0 2.8 %branch_0_fun.8 = (bf16[136,768]{1,0:T(8,128)(2,1)S(1)}, bf16[128,768]{1,0:T(8,128)(2,1)S(1)}) custom-call(bf16[136,768]{1,0:T(8,128)(2,1)S(1)} %get-tuple-element.18.marks_ref.refs_0_, bf16[136,768]{1,0:T(8,128)(2,1)S(1)} %get-tuple-element.19.marks_ref.refs_1_, bf16[128,768]{1,0:T(8,128)(2,1)S(1)} %collective-permute-done.refs_2_, ...), custom_call_target="tpu_custom_call" | custom-call | flops 1610612736 | bytes 1048576 | tf_op jit(solution)/shard_map/cond/branch_0_fun/pallas_call | solution.py:314
  15.8 2.5 %collective-permute-start.3 = (bf16[136,768]{1,0:T(8,128)(2,1)S(1)}, bf16[136,768]{1,0:T(8,128)(2,1)S(1)}, u32[]{:S(2)}, u32[]{:S(2)}) collective-permute-start(bf16[136,768]{1,0:T(8,128)(2,1)S(1)} %get-tuple-element.32.one), channel_id=1, source_target_pairs={{0,2},{1,5},{2,0},{3,7},{4,6},{5,1},{6,4},{7,3},{8,10},{9,13},{10,... | collective-permute-start | bytes 626696 | tf_op jit(solution)/shard_map/cond/branch_0_fun/ppermute | solution.py:218
  18.4 3.8 %collective-permute-done.3.two = bf16[136,768]{1,0:T(8,128)(2,1)S(1)} collective-permute-done((bf16[136,768]{1,0:T(8,128)(2,1)S(1)}, bf16[136,768]{1,0:T(8,128)(2,1)S(1)}, u32[]{:S(2)}, u32[]{:S(2)}) %collective-permute-start.3) | collective-permute-done | bytes 208928 | tf_op jit(solution)/shard_map/cond/branch_0_fun/ppermute | solution.py:218
  22.1 0.1 branch_0_fun.9.one
  22.2 2.4 %collective-permute-start.4 = (bf16[136,768]{1,0:T(8,128)(2,1)S(1)}, bf16[136,768]{1,0:T(8,128)(2,1)S(1)}, u32[]{:S(2)}, u32[]{:S(2)}) collective-permute-start(bf16[136,768]{1,0:T(8,128)(2,1)S(1)} %branch_0_fun.9.one), channel_id=1, source_target_pairs={{0,4},{1,3},{2,6},{3,1},{4,0},{5,7},{6,2},{7,5},{8,12},{9,11},{10,... | collective-permute-start | bytes 626696 | tf_op jit(solution)/shard_map/cond/branch_0_fun/ppermute | solution.py:218
  24.6 3.8 %collective-permute-done.4.two = bf16[136,768]{1,0:T(8,128)(2,1)S(1)} collective-permute-done((bf16[136,768]{1,0:T(8,128)(2,1)S(1)}, bf16[136,768]{1,0:T(8,128)(2,1)S(1)}, u32[]{:S(2)}, u32[]{:S(2)}) %collective-permute-start.4) | collective-permute-done | bytes 208928 | tf_op jit(solution)/shard_map/cond/branch_0_fun/ppermute | solution.py:218
  28.4 2.5 %branch_0_fun.10 = (bf16[136,768]{1,0:T(8,128)(2,1)S(1)}, f32[128,768]{1,0:T(8,128)S(1)}) custom-call(bf16[128,768]{1,0:T(8,128)(2,1)S(1)} %get-tuple-element.31.before_ref, bf16[136,768]{1,0:T(8,128)(2,1)S(1)} %branch_0_fun.9.one, bf16[136,768]{1,0:T(8,128)(2,1)S(1)} %collective-permute-done.4.two, ...), custom_call_target="tpu_custom_call" | custom-call | flops 1610612736 | bytes 1048576 | tf_op jit(solution)/shard_map/cond/branch_0_fun/pallas_call | solution.py:314
  30.9 1.7 %collective-permute-start.5 = (bf16[136,768]{1,0:T(8,128)(2,1)S(1)}, bf16[136,768]{1,0:T(8,128)(2,1)S(1)}, u32[]{:S(2)}, u32[]{:S(2)}) collective-permute-start(bf16[136,768]{1,0:T(8,128)(2,1)S(1)} %get-tuple-element.34.refs_0_), channel_id=1, source_target_pairs={{0,2},{1,5},{2,3},{3,4},{4,0},{5,7},{6,1},{7,6},{8,10},{9,13},{10,... | collective-permute-start | bytes 626696 | tf_op jit(solution)/shard_map/cond/branch_0_fun/ppermute | solution.py:218
  32.6 0.0 collective-permute-start.6
  32.6 4.1 %collective-permute-done.5.refs_1_ = bf16[136,768]{1,0:T(8,128)(2,1)S(1)} collective-permute-done((bf16[136,768]{1,0:T(8,128)(2,1)S(1)}, bf16[136,768]{1,0:T(8,128)(2,1)S(1)}, u32[]{:S(2)}, u32[]{:S(2)}) %collective-permute-start.5) | collective-permute-done | bytes 208928 | tf_op jit(solution)/shard_map/cond/branch_0_fun/ppermute | solution.py:218
  36.8 2.2 %collective-permute-done.6.refs_2_ = bf16[136,768]{1,0:T(8,128)(2,1)S(1)} collective-permute-done((bf16[136,768]{1,0:T(8,128)(2,1)S(1)}, bf16[136,768]{1,0:T(8,128)(2,1)S(1)}, u32[]{:S(2)}, u32[]{:S(2)}) %collective-permute-start.6) | collective-permute-done | bytes 208928 | tf_op jit(solution)/shard_map/cond/branch_0_fun/ppermute | solution.py:218
  39.0 0.2 branch_0_fun.11
  39.4 0.1 collective-permute-start.22
  39.5 1.7 %collective-permute-done.22.two = f32[136,768]{1,0:T(8,128)S(1)} collective-permute-done((f32[136,768]{1,0:T(8,128)S(1)}, f32[136,768]{1,0:T(8,128)S(1)}, u32[]{:S(2)}, u32[]{:S(2)}) %collective-permute-start.22) | collective-permute-done | bytes 417824 | tf_op jit(solution)/shard_map/ppermute | solution.py:288
  41.2 0.9 %shard_map.60 = (f32[1,128,768]{2,1,0:T(8,128)}, f32[1,128]{1,0:T(1,128)}) custom-call(f32[136,768]{1,0:T(8,128)S(1)} %get-tuple-element.67.one, f32[136,768]{1,0:T(8,128)S(1)} %collective-permute-done.22.two), custom_call_target="tpu_custom_call" | custom-call | bytes 1048576 | tf_op jit(solution)/shard_map/pallas_call | solution.py:353
  (1 shorter events, 0.0 us)
Async XLA Ops:
  3.0 1.6 %collective-permute-start.21 = (bf16[136,768]{1,0:T(8,128)(2,1)S(1)}, bf16[136,768]{1,0:T(8,128)(2,1)S(1)}, u32[]{:S(2)}, u32[]{:S(2)}) collective-permute-start(bf16[136,768]{1,0:T(8,128)(2,1)S(1)} %get-tuple-element.65), channel_id=1, source_target_pairs={{0,1},{1,0},{2,3},{3,2},{4,5},{5,4},{6,7},{7,6},{8,9},{9,8},{10,11... | collective-permute-start | bytes 626696 | tf_op jit(solution)/shard_map/ppermute | solution.py:288
  4.6 5.8 %collective-permute-start.2 = (bf16[2048,768]{1,0:T(8,128)(2,1)S(1)}, bf16[2048,768]{1,0:T(8,128)(2,1)S(1)}, u32[]{:S(2)}, u32[]{:S(2)}) collective-permute-start(bf16[2048,768]{1,0:T(8,128)(2,1)S(1)} %get-tuple-element.24.rows_ref), channel_id=1, source_target_pairs={{0,1},{1,0},{2,3},{3,2},{4,5},{5,4},{6,7},{7,6},{8,9},{9,8},{10,11... | collective-permute-start | bytes 9437192 | tf_op jit(solution)/shard_map/cond/branch_0_fun/ppermute | solution.py:288
  5.0 8.0 %collective-permute-start = (bf16[128,768]{1,0:T(8,128)(2,1)S(1)}, bf16[128,768]{1,0:T(8,128)(2,1)S(1)}, u32[]{:S(2)}, u32[]{:S(2)}) collective-permute-start(bf16[128,768]{1,0:T(8,128)(2,1)S(1)} %slice_add_fusion), channel_id=1, source_target_pairs={{0,2},{1,4},{2,0},{3,6},{4,1},{5,7},{6,3},{7,5},{8,10},{9,12},{10,... | collective-permute-start | bytes 589832 | tf_op jit(solution)/shard_map/cond/branch_0_fun/ppermute | solution.py:218
  7.7 5.3 %collective-permute-start.1 = (bf16[128,768]{1,0:T(8,128)(2,1)S(1)}, bf16[128,768]{1,0:T(8,128)(2,1)S(1)}, u32[]{:S(2)}, u32[]{:S(2)}) collective-permute-start(bf16[128,768]{1,0:T(8,128)(2,1)S(1)} %slice_add_fusion), channel_id=1, source_target_pairs={{0,6},{1,0},{2,4},{3,2},{4,5},{5,3},{6,7},{7,1},{8,14},{9,8},{10,1... | collective-permute-start | bytes 589832 | tf_op jit(solution)/shard_map/cond/branch_0_fun/ppermute | solution.py:218
  15.8 6.3 %collective-permute-start.3 = (bf16[136,768]{1,0:T(8,128)(2,1)S(1)}, bf16[136,768]{1,0:T(8,128)(2,1)S(1)}, u32[]{:S(2)}, u32[]{:S(2)}) collective-permute-start(bf16[136,768]{1,0:T(8,128)(2,1)S(1)} %get-tuple-element.32.one), channel_id=1, source_target_pairs={{0,2},{1,5},{2,0},{3,7},{4,6},{5,1},{6,4},{7,3},{8,10},{9,13},{10,... | collective-permute-start | bytes 626696 | tf_op jit(solution)/shard_map/cond/branch_0_fun/ppermute | solution.py:218
  22.2 6.2 %collective-permute-start.4 = (bf16[136,768]{1,0:T(8,128)(2,1)S(1)}, bf16[136,768]{1,0:T(8,128)(2,1)S(1)}, u32[]{:S(2)}, u32[]{:S(2)}) collective-permute-start(bf16[136,768]{1,0:T(8,128)(2,1)S(1)} %branch_0_fun.9.one), channel_id=1, source_target_pairs={{0,4},{1,3},{2,6},{3,1},{4,0},{5,7},{6,2},{7,5},{8,12},{9,11},{10,... | collective-permute-start | bytes 626696 | tf_op jit(solution)/shard_map/cond/branch_0_fun/ppermute | solution.py:218
  30.9 5.9 %collective-permute-start.5 = (bf16[136,768]{1,0:T(8,128)(2,1)S(1)}, bf16[136,768]{1,0:T(8,128)(2,1)S(1)}, u32[]{:S(2)}, u32[]{:S(2)}) collective-permute-start(bf16[136,768]{1,0:T(8,128)(2,1)S(1)} %get-tuple-element.34.refs_0_), channel_id=1, source_target_pairs={{0,2},{1,5},{2,3},{3,4},{4,0},{5,7},{6,1},{7,6},{8,10},{9,13},{10,... | collective-permute-start | bytes 626696 | tf_op jit(solution)/shard_map/cond/branch_0_fun/ppermute | solution.py:218
  32.6 6.3 %collective-permute-start.6 = (bf16[136,768]{1,0:T(8,128)(2,1)S(1)}, bf16[136,768]{1,0:T(8,128)(2,1)S(1)}, u32[]{:S(2)}, u32[]{:S(2)}) collective-permute-start(bf16[136,768]{1,0:T(8,128)(2,1)S(1)} %get-tuple-element.34.refs_0_), channel_id=1, source_target_pairs={{0,1},{1,7},{2,0},{3,6},{4,2},{5,4},{6,3},{7,5},{8,9},{9,15},{10,8... | collective-permute-start | bytes 626696 | tf_op jit(solution)/shard_map/cond/branch_0_fun/ppermute | solution.py:218
  39.4 1.8 %collective-permute-start.22 = (f32[136,768]{1,0:T(8,128)S(1)}, f32[136,768]{1,0:T(8,128)S(1)}, u32[]{:S(2)}, u32[]{:S(2)}) collective-permute-start(f32[136,768]{1,0:T(8,128)S(1)} %get-tuple-element.67.one), channel_id=1, source_target_pairs={{0,1},{1,0},{2,3},{3,2},{4,5},{5,4},{6,7},{7,6},{8,9},{9,8},{10,11... | collective-permute-start | bytes 1253384 | tf_op jit(solution)/shard_map/ppermute | solution.py:288
where the time goes:
time: 42.4 us; the launch traced here: 42.3 us
  waiting for transfers between devices  17.5 us (41%)
  starting transfers between devices  11.8 us (28%)
  Pallas kernels  11.1 us (26%)
  between operations  1.49 us (4%)
    ppermute x6, waiting for transfers between devices, permute(): return lax.ppermute(value, AXES, pairs)  15.4 us
    ppermute x6, starting transfers between devices, permute(): return lax.ppermute(value, AXES, pairs)  10.8 us
    pallas_call x2, Pallas kernels, iteration(): call(kernel, [VMEM] * (len(inputs) + len(held)), (payload, jax.ShapeDtype...  5.32 us
    pallas_call x1, Pallas kernels, local(): call(seed_kernel, [HBM] * 3, (jax.ShapeDtypeStruct((k + TAIL, width), BF1...  2.32 us
    ppermute x3, waiting for transfers between devices, swap_cores(): lax.ppermute(value, 'sub', [(sub, sub ^ 1) for sub in range(lax.axis_size...  2.18 us
    pallas_call x1, Pallas kernels, refine(): call(partial(hold_kernel, 1, block), [VMEM] * 5, both, [VMEM] * 3, aliase...  1.2 us
    pallas_call x1, Pallas kernels, refine(): call(partial(hold_kernel, 0, block), [VMEM] * 2, both, [VMEM] * 3)  1.2 us
    ppermute x3, starting transfers between devices, swap_cores(): lax.ppermute(value, 'sub', [(sub, sub ^ 1) for sub in range(lax.axis_size...  0.96 us
  transfers between devices with their start and end apart: 9, of which 7 were waited for; matrix products, arithmetic and copies ran while one was open for 0% of the time, Pallas kernels for 6%

commit v1 on v0

--- a/solution.py
+++ b/solution.py
@@ -42,7 +42,7 @@
     return terms[0]
 
 
-def seed_kernel(index_ref, labels_ref, rows_ref, out_ref, held_ref, index, labels, sems):
+def seed_kernel(index_ref, labels_ref, rows_ref, out_ref, held_ref, index, labels, total, sems):
     chunks = sems.shape[0] - 2
     k, width = index_ref.shape[1], rows_ref.shape[1]
     rows = rows_ref.shape[0]
@@ -58,12 +58,16 @@
         copies[-1].start()
     first.wait()
     picked = column(index[...].astype(F32)).astype(jnp.int32) - lax.axis_index("sub") * rows
-    total = jnp.zeros((k, width), F32)
-    for i in range(chunks):
+    total[...] = jnp.zeros_like(total)
+
+    @pl.loop(0, chunks)
+    def _(i):
         onehot = (lax.broadcasted_iota(jnp.int32, (k, size), 1) == picked - i * size).astype(F32).astype(BF16)
-        copies[i].wait()
-        total = total + contract(onehot, held_ref[pl.ds(i * size, size), :], 1, 0)
-    out_ref[0:k, :] = total.astype(BF16)
+        span = pl.ds(pl.multiple_of(i * size, size), size)
+        pltpu.make_async_copy(rows_ref.at[span], held_ref.at[span], sems.at[i]).wait()
+        total[...] += contract(onehot, held_ref[span, :], 1, 0)
+
+    out_ref[0:k, :] = total[...].astype(BF16)
     out_ref[k : k + TAIL, :] = jnp.zeros((TAIL, width), BF16)
     second.wait()
     marks = jnp.concatenate([labels[...].astype(F32), jnp.zeros((1, LANES - labels.shape[1]), F32)], axis=1)
@@ -72,9 +76,9 @@
 
 def hold_kernel(half, block, rows_ref, marks_ref, *refs):
     held_ref, turned_ref, kept_ref = refs[-3:]
-    size = rows_ref.shape[0] // 4
-
-    @pl.loop(0, 4)
+    size = rows_ref.shape[0] // 8
+
+    @pl.loop(0, 8)
     def _(i):
         span = pl.ds(pl.multiple_of(i * size, size), size)
         part = rows_ref[span, :]
@@ -125,7 +129,7 @@
         centroids = centroids + part[0:k, :].astype(F32)
     half = centroids.astype(BF16)
     c_ref[...] = half
-    accumulate(half, held, turned, kept, out_ref, sums, counts, scale, False)
+    accumulate(half, held, turned, kept, out_ref, sums, counts, scale, True)
 
 
 def number_of(tail):
@@ -325,9 +329,14 @@
             partial(next_kernel, scale), [centroids, *plan.sums(sums)], F32
         )
     parts = plan.last_sums(sums)
-    return call(
+    share = call(
         partial(share_kernel, bit), [VMEM] * (1 + len(parts)), jax.ShapeDtypeStruct((k + TAIL, width), F32)
     )(centroids, *parts)
+    return call(
+        output_kernel, [VMEM] * 2,
+        (jax.ShapeDtypeStruct((1, k, width), F32), jax.ShapeDtypeStruct((1, k), F32)), (HBM, HBM),
+        [pltpu.VMEM((k, width), F32), pltpu.VMEM((1, k), F32), pltpu.SemaphoreType.DMA((OUT_CHUNKS + 1,))],
+    )(share, swap_cores(share))
 
 
 def local(embeddings, labels, group_bit, init_index):
@@ -340,21 +349,17 @@
         [
             pltpu.VMEM((1, k), jnp.int32),
             pltpu.VMEM((1, labels.shape[0]), jnp.int32),
+            pltpu.VMEM((k, width), F32),
             pltpu.SemaphoreType.DMA((CHUNKS + 2,)),
         ], 2 * k * rows * width, SEED_VMEM,
     )(init_index, labels[None], embeddings)
     other_marks = swap_cores(own_marks)
     block = rows // labels.shape[0]
-    share = lax.switch(
+    return lax.switch(
         group_bit[0],
         [partial(refine, bit=bit, block=block) for bit in range(levels)],
         own_marks, other_marks, own_rows,
     )
-    return call(
-        output_kernel, [VMEM] * 2,
-        (jax.ShapeDtypeStruct((1, k, width), F32), jax.ShapeDtypeStruct((1, k), F32)), (HBM, HBM),
-        [pltpu.VMEM((k, width), F32), pltpu.VMEM((1, k), F32), pltpu.SemaphoreType.DMA((OUT_CHUNKS + 1,))],
-    )(share, swap_cores(share))
 
 
 def solution(mesh):

time: 42.4 us -> 42.2 us (level)
  transfers between devices with their start and end apart: 9 -> 9, of which waited for: 7 -> 7; matrix products, arithmetic and copies ran while one was open for 0% -> 0% of each run, Pallas kernels for 6% -> 7%
where the time goes in v1:
time: 42.2 us
  waiting for transfers between devices  17.2 us (41%)
  starting transfers between devices  11.8 us (28%)
  Pallas kernels  11.2 us (27%)
  between operations  1.47 us (3%)
  loops' own time  0.47 us (1%)
    ppermute x6, waiting for transfers between devices, permute(): return lax.ppermute(value, AXES, pairs)  15 us
    ppermute x6, starting transfers between devices, permute(): return lax.ppermute(value, AXES, pairs)  10.8 us
    pallas_call x2, Pallas kernels, iteration(): call(kernel, [VMEM] * (len(inputs) + len(held)), (payload, jax.ShapeDtype...  4.9 us
    pallas_call x1, Pallas kernels, local(): call(seed_kernel, [HBM] * 3, (jax.ShapeDtypeStruct((k + TAIL, width), BF1...  2.4 us
    ppermute x3, waiting for transfers between devices, swap_cores(): lax.ppermute(value, 'sub', [(sub, sub ^ 1) for sub in range(lax.axis_size...  2.18 us
    pallas_call x1, Pallas kernels, refine(): call(partial(hold_kernel, 1, block), [VMEM] * 5, both, [VMEM] * 3, aliase...  1.41 us
    pallas_call x1, Pallas kernels, refine(): call(partial(hold_kernel, 0, block), [VMEM] * 2, both, [VMEM] * 3)  1.4 us
    ppermute x3, starting transfers between devices, swap_cores(): lax.ppermute(value, 'sub', [(sub, sub ^ 1) for sub in range(lax.axis_size...  0.96 us
  transfers between devices with their start and end apart: 9, of which 7 were waited for; matrix products, arithmetic and copies ran while one was open for 0% of the time, Pallas kernels for 7%

profile of v1, /device:TPU:0, one launch (start us, length us, event | category | flops | bytes accessed | tf_op | source)
XLA Modules:
  0.0 42.2 jit_solution(4725034937285025553)
XLA Ops:
  0.6 2.4 %shard_map.65 = (bf16[136,768]{1,0:T(8,128)(2,1)S(1)}, bf16[2048,768]{1,0:T(8,128)(2,1)S(1)}) custom-call(s32[1,128]{1,0:T(1,128)} %index_ref.1, s32[1,16]{1,0:T(1,128)} %bitcast.2, bf16[2048,768]{1,0:T(8,128)(2,1)} %rows_ref.1), custom_call_target="tpu_custom_call" | custom-call | flops 402653184 | bytes 1048576 | tf_op jit(solution)/shard_map/pallas_call | solution.py:346
  3.0 0.5 %collective-permute-start.24 = (bf16[136,768]{1,0:T(8,128)(2,1)S(1)}, bf16[136,768]{1,0:T(8,128)(2,1)S(1)}, u32[]{:S(2)}, u32[]{:S(2)}) collective-permute-start(bf16[136,768]{1,0:T(8,128)(2,1)S(1)} %get-tuple-element.61), channel_id=1, source_target_pairs={{0,1},{1,0},{2,3},{3,2},{4,5},{5,4},{6,7},{7,6},{8,9},{9,8},{10,11... | collective-permute-start | bytes 626696 | tf_op jit(solution)/shard_map/ppermute | solution.py:292
  4.2 0.4 %collective-permute-done.24 = bf16[136,768]{1,0:T(8,128)(2,1)S(1)} collective-permute-done((bf16[136,768]{1,0:T(8,128)(2,1)S(1)}, bf16[136,768]{1,0:T(8,128)(2,1)S(1)}, u32[]{:S(2)}, u32[]{:S(2)}) %collective-permute-start.24) | collective-permute-done | bytes 208928 | tf_op jit(solution)/shard_map/ppermute | solution.py:292
  4.6 37.4 %conditional.1 = ((f32[1,128,768]{2,1,0:T(8,128)}, f32[1,128]{1,0:T(1,128)})) conditional(s32[]{:T(128)} %bitcast, (bf16[136,768]{1,0:T(8,128)(2,1)S(1)}, bf16[136,768]{1,0:T(8,128)(2,1)S(1)}, bf16[2048,768]{1,0:T(8,128)(2,1)S(1)}) %tuple.16, (bf16[136,768]{1,0:T(8,128)(2,1)S(1)}, bf16[136,768]{1,0:T(8,128)(2,1)S(1)}, ...), branch_computations={%region_0.0_spmd, %region_1.0_spmd, %region_2.0_spmd} | conditional | flops 3221323776 | bytes 27099464 | solution.py:358
  4.6 0.4 collective-permute-start.10
  5.0 2.7 %collective-permute-start.8 = (bf16[128,768]{1,0:T(8,128)(2,1)S(1)}, bf16[128,768]{1,0:T(8,128)(2,1)S(1)}, u32[]{:S(2)}, u32[]{:S(2)}) collective-permute-start(bf16[128,768]{1,0:T(8,128)(2,1)S(1)} %slice_add_fusion.1), channel_id=1, source_target_pairs={{0,2},{1,8},{2,0},{3,10},{4,6},{5,12},{6,4},{7,14},{8,1},{9,11},{1... | collective-permute-start | bytes 589832 | tf_op jit(solution)/shard_map/cond/branch_1_fun/ppermute | solution.py:222
  7.8 1.4 %collective-permute-start.9 = (bf16[128,768]{1,0:T(8,128)(2,1)S(1)}, bf16[128,768]{1,0:T(8,128)(2,1)S(1)}, u32[]{:S(2)}, u32[]{:S(2)}) collective-permute-start(bf16[128,768]{1,0:T(8,128)(2,1)S(1)} %slice_add_fusion.1), channel_id=1, source_target_pairs={{0,10},{1,0},{2,8},{3,2},{4,14},{5,4},{6,12},{7,6},{8,9},{9,3},{10... | collective-permute-start | bytes 589832 | tf_op jit(solution)/shard_map/cond/branch_1_fun/ppermute | solution.py:222
  9.2 1.4 %branch_1_fun.7 = (bf16[2,2048,768]{2,1,0:T(8,128)(2,1)S(1)}, bf16[2,768,2048]{2,1,0:T(8,128)(2,1)S(1)}, f32[2,8,2048]{2,1,0:T(8,128)S(1)}) custom-call(bf16[2048,768]{1,0:T(8,128)(2,1)S(1)} %get-tuple-element.33.rows_ref, bf16[136,768]{1,0:T(8,128)(2,1)S(1)} %get-tuple-element.31.marks_ref.refs_0_), custom_call_target="tpu_custom_call" | custom-call | bytes 1048576 | tf_op jit(solution)/shard_map/cond/branch_1_fun/pallas_call | solution.py:311
  10.6 0.0 collective-permute-done.10.rows_ref
  10.6 1.4 %branch_1_fun.8 = (bf16[2,2048,768]{2,1,0:T(8,128)(2,1)S(1)}, bf16[2,768,2048]{2,1,0:T(8,128)(2,1)S(1)}, f32[2,8,2048]{2,1,0:T(8,128)S(1)}) custom-call(bf16[2048,768]{1,0:T(8,128)(2,1)S(1)} %collective-permute-done.10.rows_ref, bf16[136,768]{1,0:T(8,128)(2,1)S(1)} %get-tuple-element.32.marks_ref.refs_1_, ...), custom_call_target="tpu_custom_call", output_to_operand_aliasing={{0}: (2, {}), {1}: (3, {}), {2}: (4, {})} | custom-call | bytes 1048576 | tf_op jit(solution)/shard_map/cond/branch_1_fun/pallas_call | solution.py:312
  12.0 1.1 %collective-permute-done.8.refs_2_ = bf16[128,768]{1,0:T(8,128)(2,1)S(1)} collective-permute-done((bf16[128,768]{1,0:T(8,128)(2,1)S(1)}, bf16[128,768]{1,0:T(8,128)(2,1)S(1)}, u32[]{:S(2)}, u32[]{:S(2)}) %collective-permute-start.8) | collective-permute-done | bytes 196640 | tf_op jit(solution)/shard_map/cond/branch_1_fun/ppermute | solution.py:222
  13.1 0.0 collective-permute-done.9.refs_3_
  13.1 2.4 %branch_1_fun.9 = (bf16[136,768]{1,0:T(8,128)(2,1)S(1)}, bf16[128,768]{1,0:T(8,128)(2,1)S(1)}) custom-call(bf16[136,768]{1,0:T(8,128)(2,1)S(1)} %get-tuple-element.31.marks_ref.refs_0_, bf16[136,768]{1,0:T(8,128)(2,1)S(1)} %get-tuple-element.32.marks_ref.refs_1_, bf16[128,768]{1,0:T(8,128)(2,1)S(1)} %collective-permute-done.8.refs_2_, ...), custom_call_target="tpu_custom_call" | custom-call | flops 1610612736 | bytes 1048576 | tf_op jit(solution)/shard_map/cond/branch_1_fun/pallas_call | solution.py:318
  15.5 2.5 %collective-permute-start.11 = (bf16[136,768]{1,0:T(8,128)(2,1)S(1)}, bf16[136,768]{1,0:T(8,128)(2,1)S(1)}, u32[]{:S(2)}, u32[]{:S(2)}) collective-permute-start(bf16[136,768]{1,0:T(8,128)(2,1)S(1)} %get-tuple-element.41.one), channel_id=1, source_target_pairs={{0,2},{1,9},{2,0},{3,11},{4,6},{5,13},{6,4},{7,15},{8,10},{9,1},{1... | collective-permute-start | bytes 626696 | tf_op jit(solution)/shard_map/cond/branch_1_fun/ppermute | solution.py:222
  18.0 3.8 %collective-permute-done.11.two = bf16[136,768]{1,0:T(8,128)(2,1)S(1)} collective-permute-done((bf16[136,768]{1,0:T(8,128)(2,1)S(1)}, bf16[136,768]{1,0:T(8,128)(2,1)S(1)}, u32[]{:S(2)}, u32[]{:S(2)}) %collective-permute-start.11) | collective-permute-done | bytes 208928 | tf_op jit(solution)/shard_map/cond/branch_1_fun/ppermute | solution.py:222
  21.8 0.1 branch_1_fun.10.one
  21.9 2.5 %collective-permute-start.12 = (bf16[136,768]{1,0:T(8,128)(2,1)S(1)}, bf16[136,768]{1,0:T(8,128)(2,1)S(1)}, u32[]{:S(2)}, u32[]{:S(2)}) collective-permute-start(bf16[136,768]{1,0:T(8,128)(2,1)S(1)} %branch_1_fun.10.one), channel_id=1, source_target_pairs={{0,8},{1,3},{2,10},{3,1},{4,12},{5,7},{6,14},{7,5},{8,0},{9,11},{1... | collective-permute-start | bytes 626696 | tf_op jit(solution)/shard_map/cond/branch_1_fun/ppermute | solution.py:222
  24.4 3.8 %collective-permute-done.12.two = bf16[136,768]{1,0:T(8,128)(2,1)S(1)} collective-permute-done((bf16[136,768]{1,0:T(8,128)(2,1)S(1)}, bf16[136,768]{1,0:T(8,128)(2,1)S(1)}, u32[]{:S(2)}, u32[]{:S(2)}) %collective-permute-start.12) | collective-permute-done | bytes 208928 | tf_op jit(solution)/shard_map/cond/branch_1_fun/ppermute | solution.py:222
  28.2 2.5 %branch_1_fun.11 = (bf16[136,768]{1,0:T(8,128)(2,1)S(1)}, f32[128,768]{1,0:T(8,128)S(1)}) custom-call(bf16[128,768]{1,0:T(8,128)(2,1)S(1)} %get-tuple-element.40.before_ref, bf16[136,768]{1,0:T(8,128)(2,1)S(1)} %branch_1_fun.10.one, bf16[136,768]{1,0:T(8,128)(2,1)S(1)} %collective-permute-done.12.two, ...), custom_call_target="tpu_custom_call" | custom-call | flops 1610612736 | bytes 1048576 | tf_op jit(solution)/shard_map/cond/branch_1_fun/pallas_call | solution.py:318
  30.7 1.6 %collective-permute-start.13 = (bf16[136,768]{1,0:T(8,128)(2,1)S(1)}, bf16[136,768]{1,0:T(8,128)(2,1)S(1)}, u32[]{:S(2)}, u32[]{:S(2)}) collective-permute-start(bf16[136,768]{1,0:T(8,128)(2,1)S(1)} %get-tuple-element.43.refs_0_), channel_id=1, source_target_pairs={{0,2},{1,9},{2,3},{3,8},{4,6},{5,13},{6,7},{7,12},{8,0},{9,11},{10... | collective-permute-start | bytes 626696 | tf_op jit(solution)/shard_map/cond/branch_1_fun/ppermute | solution.py:222
  32.3 0.0 collective-permute-start.14
  32.3 4.2 %collective-permute-done.13.refs_1_ = bf16[136,768]{1,0:T(8,128)(2,1)S(1)} collective-permute-done((bf16[136,768]{1,0:T(8,128)(2,1)S(1)}, bf16[136,768]{1,0:T(8,128)(2,1)S(1)}, u32[]{:S(2)}, u32[]{:S(2)}) %collective-permute-start.13) | collective-permute-done | bytes 208928 | tf_op jit(solution)/shard_map/cond/branch_1_fun/ppermute | solution.py:222
  36.5 2.2 %collective-permute-done.14.refs_2_ = bf16[136,768]{1,0:T(8,128)(2,1)S(1)} collective-permute-done((bf16[136,768]{1,0:T(8,128)(2,1)S(1)}, bf16[136,768]{1,0:T(8,128)(2,1)S(1)}, u32[]{:S(2)}, u32[]{:S(2)}) %collective-permute-start.14) | collective-permute-done | bytes 208928 | tf_op jit(solution)/shard_map/cond/branch_1_fun/ppermute | solution.py:222
  38.7 0.2 branch_1_fun.12.one
  38.9 0.1 collective-permute-start.15
  39.0 1.7 %collective-permute-done.15.two = f32[136,768]{1,0:T(8,128)S(1)} collective-permute-done((f32[136,768]{1,0:T(8,128)S(1)}, f32[136,768]{1,0:T(8,128)S(1)}, u32[]{:S(2)}, u32[]{:S(2)}) %collective-permute-start.15) | collective-permute-done | bytes 417824 | tf_op jit(solution)/shard_map/cond/branch_1_fun/ppermute | solution.py:292
  40.7 0.9 %branch_1_fun.13 = (f32[1,128,768]{2,1,0:T(8,128)}, f32[1,128]{1,0:T(1,128)}) custom-call(f32[136,768]{1,0:T(8,128)S(1)} %branch_1_fun.12.one, f32[136,768]{1,0:T(8,128)S(1)} %collective-permute-done.15.two), custom_call_target="tpu_custom_call" | custom-call | bytes 1048576 | tf_op jit(solution)/shard_map/cond/branch_1_fun/pallas_call | solution.py:335
  (1 shorter events, 0.0 us)
Async XLA Ops:
  3.0 1.6 %collective-permute-start.24 = (bf16[136,768]{1,0:T(8,128)(2,1)S(1)}, bf16[136,768]{1,0:T(8,128)(2,1)S(1)}, u32[]{:S(2)}, u32[]{:S(2)}) collective-permute-start(bf16[136,768]{1,0:T(8,128)(2,1)S(1)} %get-tuple-element.61), channel_id=1, source_target_pairs={{0,1},{1,0},{2,3},{3,2},{4,5},{5,4},{6,7},{7,6},{8,9},{9,8},{10,11... | collective-permute-start | bytes 626696 | tf_op jit(solution)/shard_map/ppermute | solution.py:292
  4.6 6.0 %collective-permute-start.10 = (bf16[2048,768]{1,0:T(8,128)(2,1)S(1)}, bf16[2048,768]{1,0:T(8,128)(2,1)S(1)}, u32[]{:S(2)}, u32[]{:S(2)}) collective-permute-start(bf16[2048,768]{1,0:T(8,128)(2,1)S(1)} %get-tuple-element.33.rows_ref), channel_id=1, source_target_pairs={{0,1},{1,0},{2,3},{3,2},{4,5},{5,4},{6,7},{7,6},{8,9},{9,8},{10,11... | collective-permute-start | bytes 9437192 | tf_op jit(solution)/shard_map/cond/branch_1_fun/ppermute | solution.py:292
  5.0 8.0 %collective-permute-start.8 = (bf16[128,768]{1,0:T(8,128)(2,1)S(1)}, bf16[128,768]{1,0:T(8,128)(2,1)S(1)}, u32[]{:S(2)}, u32[]{:S(2)}) collective-permute-start(bf16[128,768]{1,0:T(8,128)(2,1)S(1)} %slice_add_fusion.1), channel_id=1, source_target_pairs={{0,2},{1,8},{2,0},{3,10},{4,6},{5,12},{6,4},{7,14},{8,1},{9,11},{1... | collective-permute-start | bytes 589832 | tf_op jit(solution)/shard_map/cond/branch_1_fun/ppermute | solution.py:222
  7.8 5.3 %collective-permute-start.9 = (bf16[128,768]{1,0:T(8,128)(2,1)S(1)}, bf16[128,768]{1,0:T(8,128)(2,1)S(1)}, u32[]{:S(2)}, u32[]{:S(2)}) collective-permute-start(bf16[128,768]{1,0:T(8,128)(2,1)S(1)} %slice_add_fusion.1), channel_id=1, source_target_pairs={{0,10},{1,0},{2,8},{3,2},{4,14},{5,4},{6,12},{7,6},{8,9},{9,3},{10... | collective-permute-start | bytes 589832 | tf_op jit(solution)/shard_map/cond/branch_1_fun/ppermute | solution.py:222
  15.5 6.3 %collective-permute-start.11 = (bf16[136,768]{1,0:T(8,128)(2,1)S(1)}, bf16[136,768]{1,0:T(8,128)(2,1)S(1)}, u32[]{:S(2)}, u32[]{:S(2)}) collective-permute-start(bf16[136,768]{1,0:T(8,128)(2,1)S(1)} %get-tuple-element.41.one), channel_id=1, source_target_pairs={{0,2},{1,9},{2,0},{3,11},{4,6},{5,13},{6,4},{7,15},{8,10},{9,1},{1... | collective-permute-start | bytes 626696 | tf_op jit(solution)/shard_map/cond/branch_1_fun/ppermute | solution.py:222
  21.9 6.3 %collective-permute-start.12 = (bf16[136,768]{1,0:T(8,128)(2,1)S(1)}, bf16[136,768]{1,0:T(8,128)(2,1)S(1)}, u32[]{:S(2)}, u32[]{:S(2)}) collective-permute-start(bf16[136,768]{1,0:T(8,128)(2,1)S(1)} %branch_1_fun.10.one), channel_id=1, source_target_pairs={{0,8},{1,3},{2,10},{3,1},{4,12},{5,7},{6,14},{7,5},{8,0},{9,11},{1... | collective-permute-start | bytes 626696 | tf_op jit(solution)/shard_map/cond/branch_1_fun/ppermute | solution.py:222
  30.7 5.9 %collective-permute-start.13 = (bf16[136,768]{1,0:T(8,128)(2,1)S(1)}, bf16[136,768]{1,0:T(8,128)(2,1)S(1)}, u32[]{:S(2)}, u32[]{:S(2)}) collective-permute-start(bf16[136,768]{1,0:T(8,128)(2,1)S(1)} %get-tuple-element.43.refs_0_), channel_id=1, source_target_pairs={{0,2},{1,9},{2,3},{3,8},{4,6},{5,13},{6,7},{7,12},{8,0},{9,11},{10... | collective-permute-start | bytes 626696 | tf_op jit(solution)/shard_map/cond/branch_1_fun/ppermute | solution.py:222
  32.3 6.4 %collective-permute-start.14 = (bf16[136,768]{1,0:T(8,128)(2,1)S(1)}, bf16[136,768]{1,0:T(8,128)(2,1)S(1)}, u32[]{:S(2)}, u32[]{:S(2)}) collective-permute-start(bf16[136,768]{1,0:T(8,128)(2,1)S(1)} %get-tuple-element.43.refs_0_), channel_id=1, source_target_pairs={{0,1},{1,11},{2,0},{3,10},{4,5},{5,15},{6,4},{7,14},{8,2},{9,8},{1... | collective-permute-start | bytes 626696 | tf_op jit(solution)/shard_map/cond/branch_1_fun/ppermute | solution.py:222
  38.9 1.8 %collective-permute-start.15 = (f32[136,768]{1,0:T(8,128)S(1)}, f32[136,768]{1,0:T(8,128)S(1)}, u32[]{:S(2)}, u32[]{:S(2)}) collective-permute-start(f32[136,768]{1,0:T(8,128)S(1)} %branch_1_fun.12.one), channel_id=1, source_target_pairs={{0,1},{1,0},{2,3},{3,2},{4,5},{5,4},{6,7},{7,6},{8,9},{9,8},{10,11... | collective-permute-start | bytes 1253384 | tf_op jit(solution)/shard_map/cond/branch_1_fun/ppermute | solution.py:292
